TPU v7x, 32 devices: a whole 2x2x4 slice. The times are simulated.
32 devices in a mesh: fsdp: 8 (over z, y), seq: 4 (over x, core).
Axes of the slice: x: 2, y: 2, z: 4, core: 2. Of those that a mesh axis runs over, the one named last changes fastest.
Arguments:
- tokens: bfloat16 [16, 1024, 1024], P('fsdp', 'seq'), may hold values from -6 to 6
- first_gain: float32 [1024], replicated, may hold values from 0.5 to 1.5
- first_shift: float32 [1024], replicated, may hold values from -1 to 1
- attention_weight: bfloat16 [1024, 3072], P('fsdp', 'seq'), may hold values from -0.25 to 0.25
- attention_bias: float32 [3072], replicated, may hold values from -1.5 to 1.5
- output_weight: bfloat16 [1024, 1024], P('fsdp', 'seq'), may hold values from -1.5 to 1.5
- output_bias: float32 [1024], replicated, may hold values from -1 to 1
- second_gain: float32 [1024], replicated, may hold values from 0.5 to 1.5
- second_shift: float32 [1024], replicated, may hold values from -1 to 1
- expand_weight: bfloat16 [1024, 4096], P('fsdp', 'seq'), may hold values from -0.1875 to 0.1875
- expand_bias: float32 [4096], replicated, may hold values from -1 to 1
- contract_weight: bfloat16 [4096, 1024], P('fsdp', 'seq'), may hold values from -0.1875 to 0.1875
- contract_bias: float32 [1024], replicated, may hold values from -1 to 1
- cotangent: bfloat16 [16, 1024, 1024], P('fsdp', 'seq'), may hold values from -6 to 6
- threshold: float32 [1], replicated, may hold values from 3 to 6
Outputs:
- block_output: bfloat16 [16, 1024, 1024], P('fsdp', 'seq')
- input_grad: float32 [16, 1024, 1024], P('fsdp', 'seq')
- grad_first_gain: float32 [1024], replicated
- grad_first_shift: float32 [1024], replicated
- grad_attention_weight: float32 [1024, 3072], P('fsdp', 'seq')
- grad_attention_bias: float32 [3072], replicated
- grad_output_weight: float32 [1024, 1024], P('fsdp', 'seq')
- grad_output_bias: float32 [1024], replicated
- grad_second_gain: float32 [1024], replicated
- grad_second_shift: float32 [1024], replicated
- grad_expand_weight: float32 [1024, 4096], P('fsdp', 'seq')
- grad_expand_bias: float32 [4096], replicated
- grad_contract_weight: float32 [4096, 1024], P('fsdp', 'seq')
- grad_contract_bias: float32 [1024], replicated
- head_peak: float32 [16], P('seq')
- clipped_weight: float32 [1024, 3072], P('fsdp', 'seq')
- clipped_bias: float32 [3072], P('seq')
All inputs are finite; a program needn't handle non-finite values.
Results may differ from a plain program's by a relative error of at most 0.018.
Values may be sent and summed in bfloat16 or wider, within the bound.
No kernel may reach another device: no remote copies, remote signals or barrier semaphores. Data moves between devices by JAX's collectives and lax.ppermute only.
A program may use at most 320 MiB of HBM per device.

v0:
```python
import jax
import jax.numpy as jnp
from jax import lax
from jax.sharding import PartitionSpec as P

D = 1024
H = 16
HD = 64
QBLK = 512


def layer_norm(values, gain, shift):
    centered = values - jnp.mean(values, axis=-1, keepdims=True)
    variance = jnp.mean(centered * centered, axis=-1, keepdims=True)
    return centered * lax.rsqrt(variance + 1e-05) * gain + shift


def gelu_tanh(values):
    return jax.nn.gelu(values, approximate=True)


def causal_mask(row_start, row_stop):
    row_ids = row_start + jnp.arange(row_stop - row_start)[:, None]
    col_ids = jnp.arange(row_stop)[None, :]
    return col_ids <= row_ids


def block_logits(query_block, keys_part, row_start, row_stop, logit_scale):
    logits = (
        jnp.einsum("nqhd,nkhd->nhqk", query_block, keys_part, preferred_element_type=jnp.float32)
        * logit_scale
    )
    return jnp.where(causal_mask(row_start, row_stop), logits, -jnp.inf)


def split_packed(packed):
    head_size = packed.shape[-1] // 3
    return (
        packed[..., :head_size],
        packed[..., head_size : 2 * head_size],
        packed[..., 2 * head_size :],
    )


def attend_forward(packed):
    queries, keys_all, values_all = split_packed(packed)
    length = packed.shape[1]
    logit_scale = queries.shape[-1] ** (-0.5)
    outputs = []
    log_sums = []
    peak_value = None
    for block_index in range(length // QBLK):
        row_start = block_index * QBLK
        row_stop = row_start + QBLK
        logits = block_logits(
            queries[:, row_start:row_stop], keys_all[:, :row_stop], row_start, row_stop, logit_scale
        )
        row_top = jnp.max(logits, axis=-1, keepdims=True)
        shifted = jnp.exp(logits - row_top)
        row_total = jnp.sum(shifted, axis=-1, keepdims=True)
        probabilities = (shifted / row_total).astype(jnp.bfloat16)
        block_out = jnp.einsum(
            "nhqk,nkhd->nqhd",
            probabilities,
            values_all[:, :row_stop],
            preferred_element_type=jnp.float32,
        )
        outputs.append(block_out.astype(jnp.bfloat16))
        log_sums.append((row_top + jnp.log(row_total))[..., 0])
        block_peak = jnp.max(row_top[..., 0], axis=-1)
        peak_value = block_peak if peak_value is None else jnp.maximum(peak_value, block_peak)
    return (jnp.concatenate(outputs, axis=1), jnp.concatenate(log_sums, axis=-1), peak_value)


def attend_items(packed):
    attended, log_sums, peak_value = attend_forward(packed)
    returned = lax.all_to_all(attended, "seq", split_axis=1, concat_axis=2, tiled=True)
    return (returned, log_sums, peak_value, packed)


def attend_backward(packed, log_sums, heads_cot):
    queries, keys_all, values_all = split_packed(packed)
    length = packed.shape[1]
    logit_scale = queries.shape[-1] ** (-0.5)
    query_grads = []
    key_grad = jnp.zeros(keys_all.shape, jnp.float32)
    value_grad = jnp.zeros(values_all.shape, jnp.float32)
    for block_index in range(length // QBLK):
        row_start = block_index * QBLK
        row_stop = row_start + QBLK
        query_block = queries[:, row_start:row_stop]
        cot_block = heads_cot[:, row_start:row_stop]
        logits = block_logits(query_block, keys_all[:, :row_stop], row_start, row_stop, logit_scale)
        probabilities = jnp.exp(logits - log_sums[:, :, row_start:row_stop, None])
        prob_grad = jnp.einsum(
            "nqhd,nkhd->nhqk",
            cot_block,
            values_all[:, :row_stop],
            preferred_element_type=jnp.float32,
        )
        row_inner = jnp.sum(prob_grad * probabilities, axis=-1, keepdims=True)
        logit_grad = (probabilities * (prob_grad - row_inner)).astype(jnp.bfloat16)
        query_grads.append(
            jnp.einsum(
                "nhqk,nkhd->nqhd",
                logit_grad,
                keys_all[:, :row_stop],
                preferred_element_type=jnp.float32,
            )
            * logit_scale
        )
        key_grad = key_grad.at[:, :row_stop].add(
            jnp.einsum(
                "nhqk,nqhd->nkhd", logit_grad, query_block, preferred_element_type=jnp.float32
            )
            * logit_scale
        )
        value_grad = value_grad.at[:, :row_stop].add(
            jnp.einsum(
                "nhqk,nqhd->nkhd",
                probabilities.astype(jnp.bfloat16),
                cot_block,
                preferred_element_type=jnp.float32,
            )
        )
    joined = jnp.concatenate([jnp.concatenate(query_grads, axis=1), key_grad, value_grad], axis=-1)
    return joined.astype(jnp.bfloat16)


def body(
    tokens,
    first_gain,
    first_shift,
    attention_weight,
    attention_bias,
    output_weight,
    output_bias,
    second_gain,
    second_shift,
    expand_weight,
    expand_bias,
    contract_weight,
    contract_bias,
    cotangent,
    threshold,
):
    partial_full = (
        lax.all_gather(attention_weight, "seq", axis=1, tiled=True),
        lax.all_gather(output_weight, "seq", axis=1, tiled=True),
        lax.all_gather(expand_weight, "seq", axis=1, tiled=True),
        lax.all_gather(contract_weight, "seq", axis=1, tiled=True),
    )
    full_weights = (
        lax.all_gather(partial_full[0], "fsdp", axis=0, tiled=True),
        lax.all_gather(partial_full[1], "fsdp", axis=0, tiled=True),
        lax.all_gather(partial_full[2], "fsdp", axis=0, tiled=True),
        lax.all_gather(partial_full[3], "fsdp", axis=0, tiled=True),
    )
    mixing_full, output_full, expand_full, contract_full = full_weights
    seq_here = tokens.shape[0]
    tok_here = tokens.shape[1]
    tokens_float = tokens.astype(jnp.float32)
    normed_first = layer_norm(tokens_float, first_gain, first_shift).astype(jnp.bfloat16)
    mixed = (
        jnp.einsum("ntd,de->nte", normed_first, mixing_full, preferred_element_type=jnp.float32)
        + attention_bias
    )
    mixed = mixed.astype(jnp.bfloat16).reshape(seq_here, tok_here, H, 3 * HD)
    returned, log_sums, peaks, packed = attend_items(
        lax.all_to_all(mixed, "seq", split_axis=2, concat_axis=1, tiled=True)
    )
    attended = returned.reshape(seq_here, tok_here, D)
    residual = (
        tokens_float
        + jnp.einsum("nte,ed->ntd", attended, output_full, preferred_element_type=jnp.float32)
        + output_bias
    )
    normed_second = layer_norm(residual, second_gain, second_shift).astype(jnp.bfloat16)
    hidden = (
        jnp.einsum("ntd,di->nti", normed_second, expand_full, preferred_element_type=jnp.float32)
        + expand_bias
    )
    active = gelu_tanh(hidden).astype(jnp.bfloat16)
    result = (
        residual
        + jnp.einsum("nti,id->ntd", active, contract_full, preferred_element_type=jnp.float32)
        + contract_bias
    )
    block_output = result.astype(jnp.bfloat16)
    cot_float = cotangent.astype(jnp.float32)
    grad_contract = jnp.einsum("nti,ntd->id", active, cotangent, preferred_element_type=jnp.float32)
    grad_contract_bias = jnp.sum(cot_float, axis=(0, 1))
    active_cot = jnp.einsum(
        "ntd,id->nti", cotangent, contract_full, preferred_element_type=jnp.float32
    )
    _, gelu_pull = jax.vjp(gelu_tanh, hidden)
    hidden_cot = gelu_pull(active_cot)[0].astype(jnp.bfloat16)
    grad_expand = jnp.einsum(
        "ntd,nti->di", normed_second, hidden_cot, preferred_element_type=jnp.float32
    )
    grad_expand_bias = jnp.sum(hidden_cot.astype(jnp.float32), axis=(0, 1))
    second_cot = jnp.einsum(
        "nti,di->ntd", hidden_cot, expand_full, preferred_element_type=jnp.float32
    )
    _, second_pull = jax.vjp(layer_norm, residual, second_gain, second_shift)
    residual_part, grad_second_gain, grad_second_shift = second_pull(second_cot)
    residual_cot = cot_float + residual_part
    branch_cot = residual_cot.astype(jnp.bfloat16)
    grad_output = jnp.einsum(
        "nte,ntd->ed", attended, branch_cot, preferred_element_type=jnp.float32
    )
    grad_output_bias = jnp.sum(branch_cot.astype(jnp.float32), axis=(0, 1))
    attended_cot = jnp.einsum(
        "ntd,ed->nte", branch_cot, output_full, preferred_element_type=jnp.float32
    )
    attended_cot = attended_cot.astype(jnp.bfloat16).reshape(seq_here, tok_here, H, HD)
    heads_cot = lax.all_to_all(attended_cot, "seq", split_axis=2, concat_axis=1, tiled=True)
    packed_cot = attend_backward(packed, log_sums, heads_cot)
    mixed_cot = lax.all_to_all(packed_cot, "seq", split_axis=1, concat_axis=2, tiled=True).reshape(
        seq_here, tok_here, 3 * D
    )
    grad_mixing = jnp.einsum(
        "ntd,nte->de", normed_first, mixed_cot, preferred_element_type=jnp.float32
    )
    grad_mixing_bias = jnp.sum(mixed_cot.astype(jnp.float32), axis=(0, 1))
    first_cot = jnp.einsum(
        "nte,de->ntd", mixed_cot, mixing_full, preferred_element_type=jnp.float32
    )
    _, first_pull = jax.vjp(layer_norm, tokens_float, first_gain, first_shift)
    token_part, grad_first_gain, grad_first_shift = first_pull(first_cot)
    input_grad = residual_cot + token_part
    summed_first = (
        lax.psum_scatter(
            grad_mixing.astype(jnp.bfloat16), "fsdp", scatter_dimension=0, tiled=True
        ).astype(jnp.float32),
        lax.psum_scatter(
            grad_output.astype(jnp.bfloat16), "fsdp", scatter_dimension=0, tiled=True
        ).astype(jnp.float32),
        lax.psum_scatter(
            grad_expand.astype(jnp.bfloat16), "fsdp", scatter_dimension=0, tiled=True
        ).astype(jnp.float32),
        lax.psum_scatter(
            grad_contract.astype(jnp.bfloat16), "fsdp", scatter_dimension=0, tiled=True
        ).astype(jnp.float32),
    )
    weight_grads = (
        lax.psum_scatter(
            summed_first[0].astype(jnp.bfloat16), "seq", scatter_dimension=1, tiled=True
        ).astype(jnp.float32),
        lax.psum_scatter(
            summed_first[1].astype(jnp.bfloat16), "seq", scatter_dimension=1, tiled=True
        ).astype(jnp.float32),
        lax.psum_scatter(
            summed_first[2].astype(jnp.bfloat16), "seq", scatter_dimension=1, tiled=True
        ).astype(jnp.float32),
        lax.psum_scatter(
            summed_first[3].astype(jnp.bfloat16), "seq", scatter_dimension=1, tiled=True
        ).astype(jnp.float32),
    )
    vector_totals = lax.psum(
        (
            grad_first_gain,
            grad_first_shift,
            grad_mixing_bias,
            grad_output_bias,
            grad_second_gain,
            grad_second_shift,
            grad_expand_bias,
            grad_contract_bias,
        ),
        ("fsdp", "seq"),
    )
    head_peak = lax.pmax(jnp.max(peaks, axis=0), "fsdp")
    rows_here = attention_weight.shape[0]
    col_width = attention_weight.shape[1]
    heads_here = head_peak.shape[0]
    head_size = col_width // (3 * heads_here)
    factor = jnp.sqrt(threshold[0] / jnp.maximum(head_peak, threshold[0]))
    multiplier = jnp.stack([factor, factor, jnp.ones_like(factor)], axis=1)
    clipped_weight = (
        attention_weight.astype(jnp.float32).reshape(rows_here, heads_here, 3, head_size)
        * multiplier[None, :, :, None]
    ).reshape(rows_here, col_width)
    bias_piece = lax.dynamic_slice_in_dim(
        attention_bias, lax.axis_index("seq") * col_width, col_width
    )
    clipped_bias = (bias_piece.reshape(heads_here, 3, head_size) * multiplier[:, :, None]).reshape(
        col_width
    )
    return (
        block_output,
        input_grad,
        vector_totals[0],
        vector_totals[1],
        weight_grads[0],
        vector_totals[2],
        weight_grads[1],
        vector_totals[3],
        vector_totals[4],
        vector_totals[5],
        weight_grads[2],
        vector_totals[6],
        weight_grads[3],
        vector_totals[7],
        head_peak,
        clipped_weight,
        clipped_bias,
    )


def solution(mesh):
    placed = (
        P("fsdp", "seq", None),
        P(),
        P(),
        P("fsdp", "seq"),
        P(),
        P("fsdp", "seq"),
        P(),
        P(),
        P(),
        P("fsdp", "seq"),
        P(),
        P("fsdp", "seq"),
        P(),
        P("fsdp", "seq", None),
        P(),
    )
    return jax.shard_map(
        body,
        mesh=mesh,
        in_specs=placed,
        out_specs=(
            P("fsdp", "seq", None),
            P("fsdp", "seq", None),
            P(),
            P(),
            P("fsdp", "seq"),
            P(),
            P("fsdp", "seq"),
            P(),
            P(),
            P(),
            P("fsdp", "seq"),
            P(),
            P("fsdp", "seq"),
            P(),
            P("seq"),
            P("fsdp", "seq"),
            P("seq"),
        ),
        check_vma=False,
    )
```

profile of v0, /device:TPU:0, one launch (start us, length us, event | category | flops | bytes accessed | tf_op | source)
XLA Modules:
  0.0 1167.2 jit_solution(12801582693143362905)
XLA Ops:
  8.8 11.7 %all_gather.24 = bf16[128,3072]{1,0:T(8,128)(2,1)} all-gather(bf16[128,768]{1,0:T(8,128)(2,1)} %param.30), channel_id=1, replica_groups=mesh['fsdp'=8,'seq'=4] {'seq'}, dimensions={1}, use_global_device_ids=true | all-gather | bytes 983040 | tf_op jit(solution)/shard_map/all_gather | solution.py:148
  20.5 8.3 all_gather.26
  30.6 18.4 %all-gather.15.cloned.1.call-done = bf16[512,1024]{1,0:T(8,128)(2,1)} async-done(((bf16[512,256]{1,0:T(8,128)(2,1)}), bf16[512,1024]{1,0:T(8,128)(2,1)}) %all-gather.15.cloned.1.call-update) | async-done | bytes 1048592 | tf_op jit(solution)/shard_map/all_gather | solution.py:151
  49.6 100.5 %all-gather.7.cloned.1.call-done = bf16[1024,3072]{1,0:T(8,128)(2,1)} async-done(((bf16[128,3072]{1,0:T(8,128)(2,1)}), bf16[1024,3072]{1,0:T(8,128)(2,1)}) %all-gather.7.cloned.1.call-update) | async-done | bytes 6291472 | tf_op jit(solution)/shard_map/all_gather | solution.py:154
  172.2 36.5 %all-to-all-done = bf16[2,256,16,192]{1,3,0,2:T(8,128)(2,1)} async-done(((bf16[2,256,16,192]{1,3,0,2:T(8,128)(2,1)}), bf16[2,256,16,192]{1,3,0,2:T(8,128)(2,1)}, u32[]{:S(2)}, u32[]{:S(2)}) %all-to-all-start) | async-done | bytes 3145760 | tf_op jit(solution)/shard_map/all_to_all | solution.py:170
  248.0 18.9 %all_to_all.66 = bf16[4,2,65536]{2,1,0:T(2,128)(2,1)} all-to-all(bf16[4,2,65536]{2,1,0:T(2,128)(2,1)} %reshape.309), channel_id=1, replica_groups=mesh['fsdp'=8,'seq'=4] {'seq'}, dimensions={0} | all-to-all | bytes 2097152 | tf_op jit(solution)/shard_map/all_to_all | solution.py:77
  276.3 48.9 %all-gather.13.cloned.1.call-done = bf16[1024,4096]{1,0:T(8,128)(2,1)} async-done(((bf16[128,4096]{1,0:T(8,128)(2,1)}), bf16[1024,4096]{1,0:T(8,128)(2,1)}) %all-gather.13.cloned.1.call-update) | async-done | bytes 8388624 | tf_op jit(solution)/shard_map/all_gather | solution.py:156
  325.2 10.2 fusion.17
  335.4 114.9 %all-gather.17.cloned.1.call-done = bf16[4096,1024]{1,0:T(8,128)(2,1)} async-done(((bf16[512,1024]{1,0:T(8,128)(2,1)}), bf16[4096,1024]{1,0:T(8,128)(2,1)}) %all-gather.17.cloned.1.call-update) | async-done | bytes 8388624 | tf_op jit(solution)/shard_map/all_gather | solution.py:157
  450.4 14.6 %convert_reduce_fusion = (f32[4096]{0:T(1024)}, bf16[2,256,4096]{2,1,0:T(8,128)(2,1)S(1)}) fusion(f32[2,256,4096]{2,1,0:T(8,128)} %fusion.17, f32[4096]{0:T(1024)S(1)} %copy-done.41, bf16[2,256,1024]{2,1,0:T(8,128)(2,1)} %param.40, bf16[4096,1024]{1,0:T(8,128)(2,1)} %all-gather.17.cloned.1.call-done), kind=kOutput, calls=%fused_computation.29 | convolution fusion | flops 4343197696 | bytes 22052864 | tf_op jit(solution)/shard_map/ntd,id->nti/dot_general | solution.py:193
  486.9 9.9 all-to-all-done.2
  526.2 10.9 fusion.98
  567.6 53.8 %all_to_all.67 = bf16[2,1024,4,192]{3,2,0,1:T(4,128)(2,1)} all-to-all(bf16[2,1024,4,192]{3,2,0,1:T(4,128)(2,1)} %copy.170), channel_id=1, replica_groups=mesh['fsdp'=8,'seq'=4] {'seq'}, dimensions={1} | all-to-all | bytes 6291456 | tf_op jit(solution)/shard_map/all_to_all | solution.py:219
  637.7 13.1 %bitcast_convert_fusion = bf16[4096,1024]{1,0:T(8,128)(2,1)} fusion(bf16[2,256,1024]{2,1,0:T(8,128)(2,1)S(1)} %copy-done.12, f32[2,256,4096]{2,1,0:T(8,128)} %fusion.17, f32[4096]{0:T(1024)S(1)} %copy-done.42), kind=kOutput, calls=%fused_computation | convolution fusion | flops 4320133120 | bytes 17842176 | tf_op jit(solution)/shard_map/nti,ntd->id/dot_general | solution.py:191
  652.4 9.5 bitcast_convert_fusion.1
  662.7 89.2 %reduce-scatter.9.cloned.1.call-done = bf16[128,3072]{1,0:T(8,128)(2,1)} async-done(((bf16[1024,3072]{1,0:T(8,128)(2,1)}), bf16[128,3072]{1,0:T(8,128)(2,1)}) %reduce-scatter.9.cloned.1.call-update) | async-done | bytes 786448 | tf_op jit(solution)/shard_map/reduce_scatter | solution.py:233
  752.7 151.0 %reduce-scatter.21.cloned.1.call-done = bf16[512,1024]{1,0:T(8,128)(2,1)} async-done(((bf16[4096,1024]{1,0:T(8,128)(2,1)}), bf16[512,1024]{1,0:T(8,128)(2,1)}) %reduce-scatter.21.cloned.1.call-update) | async-done | bytes 1048592 | tf_op jit(solution)/shard_map/reduce_scatter | solution.py:242
  903.8 12.2 %add_convert_fusion.1 = bf16[2,256,1024]{2,1,0:T(8,128)(2,1)} fusion(f32[2,256,1024]{2,1,0:T(8,128)S(1)} %copy-done.6, bf16[4096,1024]{1,0:T(8,128)(2,1)} %all-gather.17.cloned.1.call-done, f32[1024]{0:T(1024)S(1)} %copy-done.47, f32[2,256,4096]{2,1,0:T(8,128)} %fusion.17, f32[4096]{0:T(1024)S(1)} %copy-done.42), kind=kOutput, calls=%fused_computation.83 | convolution fusion | flops 4317511680 | bytes 19943424 | tf_op jit(solution)/shard_map/nti,id->ntd/dot_general | solution.py:186
  916.0 20.6 %pmax.7 = f32[4]{0:T(128)S(1)} all-reduce(f32[4]{0:T(128)S(1)} %maximum_reduce_fusion), channel_id=1, replica_groups=mesh['fsdp'=8,'seq'=4] {'fsdp'}, use_global_device_ids=true, to_apply=%region_41.42 | all-reduce | flops 4 | bytes 32 | tf_op jit(solution)/shard_map/pmax | solution.py:273
  939.2 8.0 copy.193
  950.7 105.3 %reduce-scatter.17.cloned.1.call-done = bf16[128,4096]{1,0:T(8,128)(2,1)} async-done(((bf16[1024,4096]{1,0:T(8,128)(2,1)}), bf16[128,4096]{1,0:T(8,128)(2,1)}) %reduce-scatter.17.cloned.1.call-update) | async-done | bytes 1048592 | tf_op jit(solution)/shard_map/reduce_scatter | solution.py:239
  1066.7 40.8 %all-reduce.2 = (f32[1024]{0:T(1024)}, f32[1024]{0:T(1024)}, f32[3072]{0:T(1024)}, f32[1024]{0:T(1024)}, f32[1024]{0:T(1024)}, /*index=5*/f32[1024]{0:T(1024)}, f32[4096]{0:T(1024)}, f32[1024]{0:T(1024)}) all-reduce(f32[1024]{0:T(1024)S(1)} %get-tuple-element.87, ...), channel_id=1, replica_groups=mesh['fsdp'=8,'seq'=4] {'fsdp','seq'}, use_global_device_ids=true, to_apply=%region_15.16 | all-reduce | flops 13312 | bytes 106496 | tf_op jit(solution)/shard_map/psum | solution.py:260
  1110.7 20.5 %reduce-scatter.23.cloned.1.call-done = bf16[512,256]{1,0:T(8,128)(2,1)} async-done(((bf16[512,1024]{1,0:T(8,128)(2,1)}), bf16[512,256]{1,0:T(8,128)(2,1)}) %reduce-scatter.23.cloned.1.call-update) | async-done | bytes 262160 | tf_op jit(solution)/shard_map/reduce_scatter | solution.py:256
  1133.0 25.7 %reduce-scatter.19.cloned.1.call-done = bf16[128,1024]{1,0:T(8,128)(2,1)} async-done(((bf16[128,4096]{1,0:T(8,128)(2,1)}), bf16[128,1024]{1,0:T(8,128)(2,1)}) %reduce-scatter.19.cloned.1.call-update) | async-done | bytes 262160 | tf_op jit(solution)/shard_map/reduce_scatter | solution.py:253
  (223 shorter events, 198.5 us)
Async XLA Ops:
  7.2 143.0 %copy-start.28 = (f32[1024]{0:T(1024)S(1)}, f32[1024]{0:T(1024)}, u32[]{:S(2)}) copy-start(f32[1024]{0:T(1024)} %param.28) | copy-start | bytes 12292
  7.2 143.0 %copy-start.39 = (f32[3072]{0:T(1024)S(1)}, f32[3072]{0:T(1024)}, u32[]{:S(2)}) copy-start(f32[3072]{0:T(1024)} %param.31) | copy-start | bytes 36868
  7.2 143.0 %copy-start.43 = (f32[1024]{0:T(1024)S(1)}, f32[1024]{0:T(1024)}, u32[]{:S(2)}) copy-start(f32[1024]{0:T(1024)} %param.29) | copy-start | bytes 12292
  7.2 23.3 %all-gather.11.cloned.1.call-start = ((), (), s32[]{:S(2)}) async-start(), calls=%async_computation.14 | async-start | bytes 1310720 | tf_op jit(solution)/shard_map/all_gather | solution.py:150
  8.0 41.0 %all-gather.15.cloned.1.call-start = ((), (), s32[]{:S(2)}) async-start(), calls=%async_computation.16 | async-start | bytes 1310720 | tf_op jit(solution)/shard_map/all_gather | solution.py:151
  8.7 141.5 %all-gather.7.cloned.1.call-start = ((), (), s32[]{:S(2)}) async-start(), calls=%async_computation.12 | async-start | bytes 7077888 | tf_op jit(solution)/shard_map/all_gather | solution.py:154
  20.5 252.2 %all-gather.9.cloned.1.call-start = ((), (), s32[]{:S(2)}) async-start(), calls=%async_computation.13 | async-start | bytes 2359296 | tf_op jit(solution)/shard_map/all_gather | solution.py:155
  28.9 296.4 %all-gather.13.cloned.1.call-start = ((), (), s32[]{:S(2)}) async-start(), calls=%async_computation.15 | async-start | bytes 9437184 | tf_op jit(solution)/shard_map/all_gather | solution.py:156
  30.5 419.8 %all-gather.17.cloned.1.call-start = ((), (), s32[]{:S(2)}) async-start(), calls=%async_computation.17 | async-start | bytes 9437184 | tf_op jit(solution)/shard_map/all_gather | solution.py:157
  49.2 108.8 %copy-start.21 = (f32[2,256]{1,0:T(2,128)}, f32[2,256]{1,0:T(2,128)S(1)}, u32[]{:S(2)}) copy-start(f32[2,256]{1,0:T(2,128)S(1)} %broadcast_multiply_fusion.1) | copy-start | bytes 6148
  166.7 42.0 %all-to-all-start = ((bf16[2,256,16,192]{1,3,0,2:T(8,128)(2,1)}), bf16[2,256,16,192]{1,3,0,2:T(8,128)(2,1)}, u32[]{:S(2)}, u32[]{:S(2)}) async-start(bf16[2,256,16,192]{1,3,0,2:T(8,128)(2,1)} %copy.156), calls=%async_computation | async-start | bytes 6291456 | tf_op jit(solution)/shard_map/all_to_all | solution.py:170
  275.9 194.5 %copy-start.5 = (f32[2,256,1024]{2,1,0:T(8,128)}, f32[2,256,1024]{2,1,0:T(8,128)S(1)}, u32[]{:S(2)}) copy-start(f32[2,256,1024]{2,1,0:T(8,128)S(1)} %get-tuple-element.111) | copy-start | bytes 6291460
  276.3 194.1 %copy-start.31 = (f32[2,256]{1,0:T(2,128)}, f32[2,256]{1,0:T(2,128)S(1)}, u32[]{:S(2)}) copy-start(f32[2,256]{1,0:T(2,128)S(1)} %fusion.97) | copy-start | bytes 6148
  276.3 174.0 %copy-start.41 = (f32[4096]{0:T(1024)S(1)}, f32[4096]{0:T(1024)}, u32[]{:S(2)}) copy-start(f32[4096]{0:T(1024)} %param.37) | copy-start | bytes 49156
  478.8 18.0 %all-to-all-start.2 = ((bf16[2,256,16,64]{1,3,0,2:T(8,128)(2,1)}), bf16[2,256,16,64]{1,3,0,2:T(8,128)(2,1)S(1)}, u32[]{:S(2)}, u32[]{:S(2)}) async-start(bf16[2,256,16,64]{1,3,0,2:T(8,128)(2,1)} %copy.165), calls=%async_computation.2 | async-start | bytes 2097152 | tf_op jit(solution)/shard_map/all_to_all | solution.py:217
  482.3 179.7 %reduce-scatter.13.cloned.1.call-start = ((), (), s32[]{:S(2)}) async-start(), calls=%async_computation.20 | async-start | bytes 2359296 | tf_op jit(solution)/shard_map/reduce_scatter | solution.py:236
  486.8 265.1 %reduce-scatter.9.cloned.1.call-start = ((), (), s32[]{:S(2)}) async-start(), calls=%async_computation.18 | async-start | bytes 7077888 | tf_op jit(solution)/shard_map/reduce_scatter | solution.py:233
  636.5 267.2 %reduce-scatter.21.cloned.1.call-start = ((), (), s32[]{:S(2)}) async-start(), calls=%async_computation.24 | async-start | bytes 9437184 | tf_op jit(solution)/shard_map/reduce_scatter | solution.py:242
  650.8 405.1 %reduce-scatter.17.cloned.1.call-start = ((), (), s32[]{:S(2)}) async-start(), calls=%async_computation.22 | async-start | bytes 9437184 | tf_op jit(solution)/shard_map/reduce_scatter | solution.py:239
  661.9 241.9 %copy-start.47 = (f32[1024]{0:T(1024)S(1)}, f32[1024]{0:T(1024)}, u32[]{:S(2)}) copy-start(f32[1024]{0:T(1024)} %param.39) | copy-start | bytes 12292
  661.9 445.6 %reduce-scatter.15.cloned.1.call-start = ((), (), s32[]{:S(2)}) async-start(), calls=%async_computation.21 | async-start | bytes 327680 | tf_op jit(solution)/shard_map/reduce_scatter | solution.py:250
  662.6 446.4 %reduce-scatter.11.cloned.1.call-start = ((), (), s32[]{:S(2)}) async-start(), calls=%async_computation.19 | async-start | bytes 983040 | tf_op jit(solution)/shard_map/reduce_scatter | solution.py:247
  751.9 379.3 %reduce-scatter.23.cloned.1.call-start = ((), (), s32[]{:S(2)}) async-start(), calls=%async_computation.25 | async-start | bytes 1310720 | tf_op jit(solution)/shard_map/reduce_scatter | solution.py:256
  903.8 255.0 %reduce-scatter.19.cloned.1.call-start = ((), (), s32[]{:S(2)}) async-start(), calls=%async_computation.23 | async-start | bytes 1310720 | tf_op jit(solution)/shard_map/reduce_scatter | solution.py:253
  (48 other events, 826.6 us)
Sparse Core Ops, SparseCore 0:
  9.6 20.8 all-gather.10
  32.0 16.8 all-gather.14
  51.1 99.0 all-gather.6
  152.2 47.6 all-gather.8
  201.8 123.4 all-gather.12
  327.2 123.0 all-gather.16
  486.9 66.2 reduce-scatter.12
  636.6 115.1 reduce-scatter.8
  755.5 148.1 reduce-scatter.20
  907.6 148.2 reduce-scatter.16
  1058.4 19.0 reduce-scatter.14
  1080.1 23.4 reduce-scatter.10
  1106.1 25.0 reduce-scatter.22
  1133.8 24.9 reduce-scatter.18
where the time goes:
time: 1170 us
  waiting for transfers between devices  725 us (62%)
  blocking collectives  154 us (13%)
  matrix products  153 us (13%)
  local copies, waits for them, and re-layouts  71.4 us (6%)
  other arithmetic  39.2 us (3%)
  between operations  15.3 us (1%)
    reduce_scatter x1, waiting for transfers between devices, body(): lax.psum_scatter(grad_contract.astype(jnp.bfloat16), 'fsdp', scatter_dime...  151 us
    all_gather x1, waiting for transfers between devices, body(): lax.all_gather(partial_full[3], 'fsdp', axis=0, tiled=True)  115 us
    reduce_scatter x1, waiting for transfers between devices, body(): lax.psum_scatter(grad_expand.astype(jnp.bfloat16), 'fsdp', scatter_dimens...  105 us
    all_gather x1, waiting for transfers between devices, body(): lax.all_gather(partial_full[0], 'fsdp', axis=0, tiled=True)  101 us
    reduce_scatter x1, waiting for transfers between devices, body(): lax.psum_scatter(grad_mixing.astype(jnp.bfloat16), 'fsdp', scatter_dimens...  89.2 us
    all_to_all x1, blocking collectives, body(): lax.all_to_all(packed_cot, 'seq', split_axis=1, concat_axis=2, tiled=True)  53.8 us
    all_gather x1, waiting for transfers between devices, body(): lax.all_gather(partial_full[2], 'fsdp', axis=0, tiled=True)  48.9 us
    psum x1, blocking collectives, body(): lax.psum((grad_first_gain, grad_first_shift, grad_mixing_bias, grad_outpu...  40.8 us
  transfers between devices with their start and end apart: 16, of which 12 were waited for; matrix products, arithmetic and copies ran while one was open for 19% of the time, Pallas kernels for 0%

commit v1 on v0

--- a/solution.py
+++ b/solution.py
@@ -7,6 +7,18 @@
 H = 16
 HD = 64
 QBLK = 512
+
+
+def gather_by_bits(x, axis, dim):
+    ways, here = (lax.axis_size(axis), lax.axis_index(axis))
+    grown, reach = (x, 1)
+    while reach < ways:
+        theirs = lax.ppermute(grown, axis, [(d, d ^ reach) for d in range(ways)])
+        mine_first = jnp.concatenate([grown, theirs], axis=dim)
+        theirs_first = jnp.concatenate([theirs, grown], axis=dim)
+        grown = jnp.where(here & reach == 0, mine_first, theirs_first)
+        reach = 2 * reach
+    return grown
 
 
 def layer_norm(values, gain, shift):
@@ -153,7 +165,7 @@
     full_weights = (
         lax.all_gather(partial_full[0], "fsdp", axis=0, tiled=True),
         lax.all_gather(partial_full[1], "fsdp", axis=0, tiled=True),
-        lax.all_gather(partial_full[2], "fsdp", axis=0, tiled=True),
+        gather_by_bits(partial_full[2], "fsdp", 0),
         lax.all_gather(partial_full[3], "fsdp", axis=0, tiled=True),
     )
     mixing_full, output_full, expand_full, contract_full = full_weights

time: 1170 us -> 1170 us (level)
  other arithmetic: 39.2 us -> 58.7 us
  blocking collectives: 154 us -> 135 us
  waiting for transfers between devices: 725 us -> 706 us
  starting transfers between devices: 9.06 us -> 21.3 us
    ppermute x0 -> x3, waiting for transfers between devices: none -> 212 us  [gather_by_bits(): theirs = lax.ppermute(grown, axis, [(d, d ^ reach) for d in range(ways)])]
    reduce_scatter x1, waiting for transfers between devices: 151 us -> 31.5 us  [body(): lax.psum_scatter(grad_contract.astype(jnp.bfloat16), 'fsdp', scatter_dime...]
    all_gather x1, waiting for transfers between devices: 115 us -> 0.01 us  [body(): lax.all_gather(partial_full[3], 'fsdp', axis=0, tiled=True)]
    all_gather x1 -> x0, waiting for transfers between devices: 48.9 us -> none  [body(): lax.all_gather(partial_full[2], 'fsdp', axis=0, tiled=True)]
    reduce_scatter x1, waiting for transfers between devices: 89.2 us -> 120 us  [body(): lax.psum_scatter(grad_mixing.astype(jnp.bfloat16), 'fsdp', scatter_dimens...]
    reduce_scatter x1, waiting for transfers between devices: 0.01 us -> 20.6 us  [body(): lax.psum_scatter(summed_first[0].astype(jnp.bfloat16), 'seq', scatter_dim...]
    reduce_scatter x1, waiting for transfers between devices: 20.5 us -> 0.01 us  [body(): lax.psum_scatter(summed_first[3].astype(jnp.bfloat16), 'seq', scatter_dim...]
    all_to_all x1 -> x0, blocking collectives: 18.9 us -> none  [attend_items(): lax.all_to_all(attended, 'seq', split_axis=1, concat_axis=2, tiled=True)]
  transfers between devices with their start and end apart: 16 -> 19, of which waited for: 12 -> 14; matrix products, arithmetic and copies ran while one was open for 19% -> 20% of each run, Pallas kernels for 0% -> 0%
where the time goes in v1:
time: 1170 us; the launch traced here: 1160 us
  waiting for transfers between devices  706 us (60%)
  matrix products  156 us (13%)
  blocking collectives  135 us (12%)
  local copies, waits for them, and re-layouts  69.5 us (6%)
  other arithmetic  58.7 us (5%)
  starting transfers between devices  21.3 us (2%)
  between operations  15.5 us (1%)
    ppermute x3, waiting for transfers between devices, gather_by_bits(): theirs = lax.ppermute(grown, axis, [(d, d ^ reach) for d in range(ways)])  212 us
    reduce_scatter x1, waiting for transfers between devices, body(): lax.psum_scatter(grad_mixing.astype(jnp.bfloat16), 'fsdp', scatter_dimens...  120 us
    reduce_scatter x1, waiting for transfers between devices, body(): lax.psum_scatter(grad_expand.astype(jnp.bfloat16), 'fsdp', scatter_dimens...  106 us
    all_gather x1, waiting for transfers between devices, body(): lax.all_gather(partial_full[0], 'fsdp', axis=0, tiled=True)  98.5 us
    all_to_all x1, blocking collectives, body(): lax.all_to_all(packed_cot, 'seq', split_axis=1, concat_axis=2, tiled=True)  53.9 us
    psum x1, blocking collectives, body(): lax.psum((grad_first_gain, grad_first_shift, grad_mixing_bias, grad_outpu...  40.8 us
    reduce_scatter x1, waiting for transfers between devices, body(): lax.psum_scatter(grad_contract.astype(jnp.bfloat16), 'fsdp', scatter_dime...  31.5 us
    all_to_all x1, waiting for transfers between devices, body(): lax.all_to_all(mixed, 'seq', split_axis=2, concat_axis=1, tiled=True)  26.1 us
  transfers between devices with their start and end apart: 19, of which 14 were waited for; matrix products, arithmetic and copies ran while one was open for 20% of the time, Pallas kernels for 0%

profile of v1, /device:TPU:0, one launch (start us, length us, event | category | flops | bytes accessed | tf_op | source)
XLA Modules:
  0.0 1162.6 jit_solution(9877676940513610236)
XLA Ops:
  8.7 11.7 %all_gather.21 = bf16[128,3072]{1,0:T(8,128)(2,1)} all-gather(bf16[128,768]{1,0:T(8,128)(2,1)} %param.30), channel_id=1, replica_groups=mesh['fsdp'=8,'seq'=4] {'seq'}, dimensions={1}, use_global_device_ids=true | all-gather | bytes 983040 | tf_op jit(solution)/shard_map/all_gather | solution.py:160
  30.6 18.3 %all-gather.10.cloned.1.call-done = bf16[128,4096]{1,0:T(8,128)(2,1)} async-done(((bf16[128,1024]{1,0:T(8,128)(2,1)}), bf16[128,4096]{1,0:T(8,128)(2,1)}) %all-gather.10.cloned.1.call-update) | async-done | bytes 1048592 | tf_op jit(solution)/shard_map/all_gather | solution.py:162
  51.0 31.9 %collective-permute-done = bf16[128,4096]{1,0:T(8,128)(2,1)} collective-permute-done((bf16[128,4096]{1,0:T(8,128)(2,1)}, bf16[128,4096]{1,0:T(8,128)(2,1)}, u32[]{:S(2)}, u32[]{:S(2)}) %collective-permute-start) | collective-permute-done | bytes 1048608 | tf_op jit(solution)/shard_map/ppermute | solution.py:16
  87.5 98.5 %all-gather.6.cloned.1.call-done = bf16[1024,3072]{1,0:T(8,128)(2,1)} async-done(((bf16[128,3072]{1,0:T(8,128)(2,1)}), bf16[1024,3072]{1,0:T(8,128)(2,1)}) %all-gather.6.cloned.1.call-update) | async-done | bytes 6291472 | tf_op jit(solution)/shard_map/all_gather | solution.py:166
  218.6 26.1 %all-to-all-done = bf16[2,256,16,192]{1,3,0,2:T(8,128)(2,1)} async-done(((bf16[2,256,16,192]{1,3,0,2:T(8,128)(2,1)}), bf16[2,256,16,192]{1,3,0,2:T(8,128)(2,1)}, u32[]{:S(2)}, u32[]{:S(2)}) %all-to-all-start) | async-done | bytes 3145760 | tf_op jit(solution)/shard_map/all_to_all | solution.py:182
  267.2 13.7 %fusion = f32[2,4,512]{2,1,0:T(4,128)S(1)} fusion(f32[2,4,512,1024]{3,2,1,0:T(8,128)S(1)} %get-tuple-element.107, f32[2,4,512]{2,1,0:T(4,128)S(1)} %get-tuple-element.106), kind=kLoop, calls=%fused_computation.8 | loop fusion | flops 8384512 | bytes 16809984 | tf_op jit(solution)/shard_map/reduce_sum | solution.py:72
  297.8 14.5 %all-to-all-done.1 = bf16[4,2,65536]{2,1,0:T(2,128)(2,1)} async-done(((bf16[4,2,65536]{2,1,0:T(2,128)(2,1)}), bf16[4,2,65536]{2,1,0:T(2,128)(2,1)}, u32[]{:S(2)}, u32[]{:S(2)}) %all-to-all-start.1) | async-done | bytes 1048608 | tf_op jit(solution)/shard_map/all_to_all | solution.py:89
  317.9 16.3 %all-gather.8.cloned.1.call-done = bf16[1024,1024]{1,0:T(8,128)(2,1)} async-done(((bf16[128,1024]{1,0:T(8,128)(2,1)}), bf16[1024,1024]{1,0:T(8,128)(2,1)}) %all-gather.8.cloned.1.call-update) | async-done | bytes 2097168 | tf_op jit(solution)/shard_map/all_gather | solution.py:167
  337.9 179.8 %collective-permute-done.2 = bf16[512,4096]{1,0:T(8,128)(2,1)} collective-permute-done((bf16[512,4096]{1,0:T(8,128)(2,1)}, bf16[512,4096]{1,0:T(8,128)(2,1)}, u32[]{:S(2)}, u32[]{:S(2)}) %collective-permute-start.2) | collective-permute-done | bytes 4194336 | tf_op jit(solution)/shard_map/ppermute | solution.py:16
  517.8 10.6 fusion.26
  528.4 13.9 %convert_reduce_fusion = (f32[4096]{0:T(1024)}, bf16[2,256,4096]{2,1,0:T(8,128)(2,1)S(1)}) fusion(f32[2,256,4096]{2,1,0:T(8,128)} %fusion.26, f32[4096]{0:T(1024)S(1)} %copy-done.45, bf16[2,256,1024]{2,1,0:T(8,128)(2,1)} %param.40, bf16[4096,1024]{1,0:T(8,128)(2,1)} %all-gather.14.cloned.1.call-done), kind=kOutput, calls=%fused_computation.27 | convolution fusion | flops 4343197696 | bytes 22052864 | tf_op jit(solution)/shard_map/ntd,id->nti/dot_general | solution.py:205
  542.4 11.6 multiply_reduce_fusion.2
  559.1 13.0 %bitcast_convert_fusion = bf16[4096,1024]{1,0:T(8,128)(2,1)} fusion(bf16[2,256,1024]{2,1,0:T(8,128)(2,1)S(1)} %copy-done.13, f32[2,256,4096]{2,1,0:T(8,128)} %fusion.26, f32[4096]{0:T(1024)S(1)} %copy-done.45), kind=kOutput, calls=%fused_computation | convolution fusion | flops 4320133120 | bytes 17842176 | tf_op jit(solution)/shard_map/nti,ntd->id/dot_general | solution.py:203
  584.0 13.7 %all-to-all-done.2 = bf16[2,256,16,64]{1,3,0,2:T(8,128)(2,1)S(1)} async-done(((bf16[2,256,16,64]{1,3,0,2:T(8,128)(2,1)}), bf16[2,256,16,64]{1,3,0,2:T(8,128)(2,1)S(1)}, u32[]{:S(2)}, u32[]{:S(2)}) %all-to-all-start.2) | async-done | bytes 1048608 | tf_op jit(solution)/shard_map/all_to_all | solution.py:229
  623.7 10.9 fusion.101
  665.4 53.9 %all_to_all.66 = bf16[2,1024,4,192]{3,2,0,1:T(4,128)(2,1)} all-to-all(bf16[2,1024,4,192]{3,2,0,1:T(4,128)(2,1)} %copy.170), channel_id=1, replica_groups=mesh['fsdp'=8,'seq'=4] {'seq'}, dimensions={1} | all-to-all | bytes 6291456 | tf_op jit(solution)/shard_map/all_to_all | solution.py:231
  745.9 31.5 %reduce-scatter.21.cloned.1.call-done = bf16[512,1024]{1,0:T(8,128)(2,1)} async-done(((bf16[4096,1024]{1,0:T(8,128)(2,1)}), bf16[512,1024]{1,0:T(8,128)(2,1)}) %reduce-scatter.21.cloned.1.call-update) | async-done | bytes 1048592 | tf_op jit(solution)/shard_map/reduce_scatter | solution.py:254
  778.2 120.2 %reduce-scatter.9.cloned.1.call-done = bf16[128,3072]{1,0:T(8,128)(2,1)} async-done(((bf16[1024,3072]{1,0:T(8,128)(2,1)}), bf16[128,3072]{1,0:T(8,128)(2,1)}) %reduce-scatter.9.cloned.1.call-update) | async-done | bytes 786448 | tf_op jit(solution)/shard_map/reduce_scatter | solution.py:245
  898.5 12.2 %add_convert_fusion.1 = bf16[2,256,1024]{2,1,0:T(8,128)(2,1)} fusion(f32[2,256,1024]{2,1,0:T(8,128)S(1)} %copy-done.6, bf16[4096,1024]{1,0:T(8,128)(2,1)} %all-gather.14.cloned.1.call-done, f32[1024]{0:T(1024)S(1)} %copy-done.51, f32[2,256,4096]{2,1,0:T(8,128)} %fusion.26, f32[4096]{0:T(1024)S(1)} %copy-done.46), kind=kOutput, calls=%fused_computation.85 | convolution fusion | flops 4317511680 | bytes 19943424 | tf_op jit(solution)/shard_map/nti,id->ntd/dot_general | solution.py:198
  910.8 20.7 %pmax.7 = f32[4]{0:T(128)S(1)} all-reduce(f32[4]{0:T(128)S(1)} %maximum_reduce_fusion), channel_id=1, replica_groups=mesh['fsdp'=8,'seq'=4] {'fsdp'}, use_global_device_ids=true, to_apply=%region_41.42 | all-reduce | flops 4 | bytes 32 | tf_op jit(solution)/shard_map/pmax | solution.py:285
  945.4 105.5 %reduce-scatter.17.cloned.1.call-done = bf16[128,4096]{1,0:T(8,128)(2,1)} async-done(((bf16[1024,4096]{1,0:T(8,128)(2,1)}), bf16[128,4096]{1,0:T(8,128)(2,1)}) %reduce-scatter.17.cloned.1.call-update) | async-done | bytes 1048592 | tf_op jit(solution)/shard_map/reduce_scatter | solution.py:251
  1061.7 40.8 %all-reduce.2 = (f32[1024]{0:T(1024)}, f32[1024]{0:T(1024)}, f32[3072]{0:T(1024)}, f32[1024]{0:T(1024)}, f32[1024]{0:T(1024)}, /*index=5*/f32[1024]{0:T(1024)}, f32[4096]{0:T(1024)}, f32[1024]{0:T(1024)}) all-reduce(f32[1024]{0:T(1024)S(1)} %get-tuple-element.87, ...), channel_id=1, replica_groups=mesh['fsdp'=8,'seq'=4] {'fsdp','seq'}, use_global_device_ids=true, to_apply=%region_15.16 | all-reduce | flops 13312 | bytes 106496 | tf_op jit(solution)/shard_map/psum | solution.py:272
  1105.8 20.6 %reduce-scatter.11.cloned.1.call-done = bf16[128,768]{1,0:T(8,128)(2,1)} async-done(((bf16[128,3072]{1,0:T(8,128)(2,1)}), bf16[128,768]{1,0:T(8,128)(2,1)}) %reduce-scatter.11.cloned.1.call-update) | async-done | bytes 196624 | tf_op jit(solution)/shard_map/reduce_scatter | solution.py:259
  1128.1 25.9 %reduce-scatter.19.cloned.1.call-done = bf16[128,1024]{1,0:T(8,128)(2,1)} async-done(((bf16[128,4096]{1,0:T(8,128)(2,1)}), bf16[128,1024]{1,0:T(8,128)(2,1)}) %reduce-scatter.19.cloned.1.call-update) | async-done | bytes 262160 | tf_op jit(solution)/shard_map/reduce_scatter | solution.py:265
  (237 shorter events, 231.3 us)
Async XLA Ops:
  7.2 23.4 %all-gather.12.cloned.1.call-start = ((), (), s32[]{:S(2)}) async-start(), calls=%async_computation.15 | async-start | bytes 1310720 | tf_op jit(solution)/shard_map/all_gather | solution.py:163
  7.9 41.0 %all-gather.10.cloned.1.call-start = ((), (), s32[]{:S(2)}) async-start(), calls=%async_computation.14 | async-start | bytes 1310720 | tf_op jit(solution)/shard_map/all_gather | solution.py:162
  8.7 177.4 %all-gather.6.cloned.1.call-start = ((), (), s32[]{:S(2)}) async-start(), calls=%async_computation.12 | async-start | bytes 7077888 | tf_op jit(solution)/shard_map/all_gather | solution.py:166
  20.5 313.7 %all-gather.8.cloned.1.call-start = ((), (), s32[]{:S(2)}) async-start(), calls=%async_computation.13 | async-start | bytes 2359296 | tf_op jit(solution)/shard_map/all_gather | solution.py:167
  28.9 499.5 %all-gather.14.cloned.1.call-start = ((), (), s32[]{:S(2)}) async-start(), calls=%async_computation.16 | async-start | bytes 9437184 | tf_op jit(solution)/shard_map/all_gather | solution.py:169
  48.9 34.0 %collective-permute-start = (bf16[128,4096]{1,0:T(8,128)(2,1)}, bf16[128,4096]{1,0:T(8,128)(2,1)}, u32[]{:S(2)}, u32[]{:S(2)}) collective-permute-start(bf16[128,4096]{1,0:T(8,128)(2,1)} %all-gather.10.cloned.1.call-done), channel_id=1, source_target_pairs={{0,4},{4,0},{8,12},{12,8},{16,20},{20,16},{24,28},{28,24},{1,5},{5... | collective-permute-start | bytes 3145736 | tf_op jit(solution)/shard_map/ppermute | solution.py:16
  86.0 123.0 %collective-permute-start.1 = (bf16[256,4096]{1,0:T(8,128)(2,1)S(1)}, bf16[256,4096]{1,0:T(8,128)(2,1)}, u32[]{:S(2)}, u32[]{:S(2)}) collective-permute-start(bf16[256,4096]{1,0:T(8,128)(2,1)S(1)} %maximum_select_fusion.2), channel_id=1, source_target_pairs={{0,8},{4,12},{8,0},{12,4},{16,24},{20,28},{24,16},{28,20},{1,9},{5... | collective-permute-start | bytes 6291464 | tf_op jit(solution)/shard_map/ppermute | solution.py:16
  202.6 42.1 %all-to-all-start = ((bf16[2,256,16,192]{1,3,0,2:T(8,128)(2,1)}), bf16[2,256,16,192]{1,3,0,2:T(8,128)(2,1)}, u32[]{:S(2)}, u32[]{:S(2)}) async-start(bf16[2,256,16,192]{1,3,0,2:T(8,128)(2,1)} %copy.156), calls=%async_computation | async-start | bytes 6291456 | tf_op jit(solution)/shard_map/all_to_all | solution.py:182
  213.9 303.9 %collective-permute-start.2 = (bf16[512,4096]{1,0:T(8,128)(2,1)}, bf16[512,4096]{1,0:T(8,128)(2,1)}, u32[]{:S(2)}, u32[]{:S(2)}) collective-permute-start(bf16[512,4096]{1,0:T(8,128)(2,1)} %maximum_select_fusion.1), channel_id=1, source_target_pairs={{0,16},{4,20},{8,24},{12,28},{16,0},{20,4},{24,8},{28,12},{1,17},{... | collective-permute-start | bytes 12582920 | tf_op jit(solution)/shard_map/ppermute | solution.py:16
  293.3 18.9 %all-to-all-start.1 = ((bf16[4,2,65536]{2,1,0:T(2,128)(2,1)}), bf16[4,2,65536]{2,1,0:T(2,128)(2,1)}, u32[]{:S(2)}, u32[]{:S(2)}) async-start(bf16[4,2,65536]{2,1,0:T(2,128)(2,1)} %reshape.309), calls=%async_computation.1 | async-start | bytes 2097152 | tf_op jit(solution)/shard_map/all_to_all | solution.py:89
  297.7 447.6 %reduce-scatter.13.cloned.1.call-start = ((), (), s32[]{:S(2)}) async-start(), calls=%async_computation.19 | async-start | bytes 2359296 | tf_op jit(solution)/shard_map/reduce_scatter | solution.py:248
  334.2 183.6 %copy-start.42 = (f32[1024]{0:T(1024)S(1)}, f32[1024]{0:T(1024)}, u32[]{:S(2)}) copy-start(f32[1024]{0:T(1024)} %param.34) | copy-start | bytes 12292
  334.2 183.6 %copy-start.49 = (f32[1024]{0:T(1024)S(1)}, f32[1024]{0:T(1024)}, u32[]{:S(2)}) copy-start(f32[1024]{0:T(1024)} %param.35) | copy-start | bytes 12292
  337.5 216.5 %copy-start.5 = (f32[2,256,1024]{2,1,0:T(8,128)}, f32[2,256,1024]{2,1,0:T(8,128)S(1)}, u32[]{:S(2)}) copy-start(f32[2,256,1024]{2,1,0:T(8,128)S(1)} %get-tuple-element.111) | copy-start | bytes 6291460
  337.9 216.1 %copy-start.36 = (f32[2,256]{1,0:T(2,128)}, f32[2,256]{1,0:T(2,128)S(1)}, u32[]{:S(2)}) copy-start(f32[2,256]{1,0:T(2,128)S(1)} %fusion.98) | copy-start | bytes 6148
  337.9 190.5 %copy-start.45 = (f32[4096]{0:T(1024)S(1)}, f32[4096]{0:T(1024)}, u32[]{:S(2)}) copy-start(f32[4096]{0:T(1024)} %param.37) | copy-start | bytes 49156
  559.1 218.3 %reduce-scatter.21.cloned.1.call-start = ((), (), s32[]{:S(2)}) async-start(), calls=%async_computation.23 | async-start | bytes 9437184 | tf_op jit(solution)/shard_map/reduce_scatter | solution.py:254
  579.8 18.0 %all-to-all-start.2 = ((bf16[2,256,16,64]{1,3,0,2:T(8,128)(2,1)}), bf16[2,256,16,64]{1,3,0,2:T(8,128)(2,1)S(1)}, u32[]{:S(2)}, u32[]{:S(2)}) async-start(bf16[2,256,16,64]{1,3,0,2:T(8,128)(2,1)} %copy.165), calls=%async_computation.2 | async-start | bytes 2097152 | tf_op jit(solution)/shard_map/all_to_all | solution.py:229
  583.3 315.1 %reduce-scatter.9.cloned.1.call-start = ((), (), s32[]{:S(2)}) async-start(), calls=%async_computation.17 | async-start | bytes 7077888 | tf_op jit(solution)/shard_map/reduce_scatter | solution.py:245
  734.5 316.5 %reduce-scatter.17.cloned.1.call-start = ((), (), s32[]{:S(2)}) async-start(), calls=%async_computation.21 | async-start | bytes 9437184 | tf_op jit(solution)/shard_map/reduce_scatter | solution.py:251
  745.3 357.2 %reduce-scatter.15.cloned.1.call-start = ((), (), s32[]{:S(2)}) async-start(), calls=%async_computation.20 | async-start | bytes 327680 | tf_op jit(solution)/shard_map/reduce_scatter | solution.py:262
  745.9 358.2 %reduce-scatter.23.cloned.1.call-start = ((), (), s32[]{:S(2)}) async-start(), calls=%async_computation.24 | async-start | bytes 1310720 | tf_op jit(solution)/shard_map/reduce_scatter | solution.py:268
  777.4 349.0 %reduce-scatter.11.cloned.1.call-start = ((), (), s32[]{:S(2)}) async-start(), calls=%async_computation.18 | async-start | bytes 983040 | tf_op jit(solution)/shard_map/reduce_scatter | solution.py:259
  898.5 255.6 %reduce-scatter.19.cloned.1.call-start = ((), (), s32[]{:S(2)}) async-start(), calls=%async_computation.22 | async-start | bytes 1310720 | tf_op jit(solution)/shard_map/reduce_scatter | solution.py:265
  (55 other events, 1705.7 us)
Sparse Core Ops, SparseCore 0:
  9.6 20.9 all-gather.11
  32.1 16.7 all-gather.9
  51.1 134.9 all-gather.5
  188.0 146.1 all-gather.7
  336.2 173.1 all-gather.13
  559.2 66.6 reduce-scatter.12
  629.5 147.8 reduce-scatter.20
  781.4 116.9 reduce-scatter.8
  902.5 148.4 reduce-scatter.16
  1053.3 19.1 reduce-scatter.14
  1075.1 25.2 reduce-scatter.22
  1102.7 23.6 reduce-scatter.10
  1129.1 24.8 reduce-scatter.18
